TPU v7x, 32 devices: a whole 2x2x4 slice. The times are simulated.
32 devices in a mesh: tensor: 4 (over z), seq: 8 (over y, x, core).
Axes of the slice: x: 2, y: 2, z: 4, core: 2. Of those that a mesh axis runs over, the one named last changes fastest.
Arguments:
- teacher_q: bfloat16 [4096, 8192], P('seq', 'tensor'), may hold values from -24 to 24
- teacher_v: bfloat16 [4096, 8192], P('seq', 'tensor'), may hold values from -24 to 24
- student_q: bfloat16 [4096, 2048], P('seq'), may hold values from -24 to 24
- student_v: bfloat16 [4096, 2048], P('seq'), may hold values from -24 to 24
Outputs:
- grad_q: bfloat16 [4096, 2048], P('seq')
- grad_v: bfloat16 [4096, 2048], P('seq')
All inputs are finite; a program needn't handle non-finite values.
Results may differ from a plain program's by a relative error of at most 0.0095.
Values may be sent and summed in bfloat16 or wider, within the bound.
A program may use at most 128 MiB of HBM per device.

v0:
```python
import jax
import jax.numpy as jnp
from jax import lax
from jax.sharding import PartitionSpec as P

HEADS = 32
SEQS = 2


def from_partner(array, axis, distance):
    return lax.ppermute(array, axis, [(i, i ^ 1 << distance) for i in range(lax.axis_size(axis))])


def head_terms(teach_query, teach_key, stud_query, stud_key, teach_dim, stud_dim):
    teach_scores = jnp.dot(
        teach_query, teach_key.T, preferred_element_type=jnp.float32
    ) * teach_dim ** (-0.5)
    stud_scores = jnp.dot(
        stud_query, stud_key.T, preferred_element_type=jnp.float32
    ) * stud_dim ** (-0.5)
    teach_prob = jax.nn.softmax(teach_scores, axis=-1)
    stud_prob = jax.nn.softmax(stud_scores, axis=-1)
    coef = (256.0 * stud_dim ** (-0.5) * (stud_prob - teach_prob)).astype(jnp.bfloat16)
    query_grad = jnp.dot(coef, stud_key, preferred_element_type=jnp.float32)
    key_grad = jnp.einsum("qk,qd->kd", coef, stud_query, preferred_element_type=jnp.float32)
    return (query_grad, key_grad)


def relate(teach_own, teach_keys, stud_own, stud_keys, per_dev, teach_dim, stud_dim):
    tok_rows = teach_own.shape[0]
    teach_query = teach_own.reshape(tok_rows, per_dev, teach_dim).transpose(1, 0, 2)
    teach_key = teach_keys.reshape(-1, per_dev, teach_dim).transpose(1, 0, 2)
    stud_query = stud_own.reshape(tok_rows, per_dev, stud_dim).transpose(1, 0, 2)
    stud_key = stud_keys.reshape(-1, per_dev, stud_dim).transpose(1, 0, 2)

    def one_head(group):
        return head_terms(group[0], group[1], group[2], group[3], teach_dim, stud_dim)

    query_grad, key_grad = lax.map(one_head, (teach_query, teach_key, stud_query, stud_key))
    return (
        query_grad.transpose(1, 0, 2).reshape(tok_rows, per_dev * stud_dim),
        key_grad.transpose(1, 0, 2).reshape(-1, per_dev * stud_dim),
    )


def shards(teacher_q, teacher_v, student_q, student_v):
    n_tensor = lax.axis_size("tensor")
    n_seq = lax.axis_size("seq")
    per_dev = HEADS // n_tensor
    group_size = n_seq // SEQS
    level_count = group_size.bit_length() - 1
    seq_index = lax.axis_index("seq")
    member = seq_index % group_size
    teach_dim = teacher_q.shape[1] // per_dev
    stud_dim = student_q.shape[1] // HEADS
    own_width = per_dev * stud_dim
    offset = lax.axis_index("tensor") * own_width
    own_q = lax.dynamic_slice_in_dim(student_q, offset, own_width, 1)
    own_v = lax.dynamic_slice_in_dim(student_v, offset, own_width, 1)
    key_tq, key_tv, key_sq, key_sv = (teacher_q, teacher_v, own_q, own_v)
    for bit_num in range(level_count):
        partner = from_partner((key_tq, key_tv, key_sq, key_sv), "seq", bit_num)
        upper_half = member // 2**bit_num % 2 == 1
        joined = []
        for mine, theirs in zip((key_tq, key_tv, key_sq, key_sv), partner):
            joined.append(
                jnp.where(
                    upper_half,
                    jnp.concatenate([theirs, mine], 0),
                    jnp.concatenate([mine, theirs], 0),
                )
            )
        key_tq, key_tv, key_sq, key_sv = joined
    q_query, q_key = relate(teacher_q, key_tq, own_q, key_sq, per_dev, teach_dim, stud_dim)
    v_query, v_key = relate(teacher_v, key_tv, own_v, key_sv, per_dev, teach_dim, stud_dim)
    returned = jnp.concatenate([q_key, v_key], axis=1)
    for bit_num in reversed(range(level_count)):
        half_rows = returned.shape[0] // 2
        upper_half = member // 2**bit_num % 2 == 1
        low_part = returned[:half_rows]
        high_part = returned[half_rows:]
        kept = jnp.where(upper_half, high_part, low_part)
        outgoing = jnp.where(upper_half, low_part, high_part)
        returned = kept + from_partner(outgoing.astype(jnp.bfloat16), "seq", bit_num).astype(
            outgoing.dtype
        )
    head_q = (q_query + returned[:, :own_width]).astype(jnp.bfloat16)
    head_v = (v_query + returned[:, own_width:]).astype(jnp.bfloat16)
    full_q, full_v = (
        lax.all_gather(head_q, "tensor", axis=1, tiled=True),
        lax.all_gather(head_v, "tensor", axis=1, tiled=True),
    )
    return (full_q, full_v)


def solution(mesh):
    in_specs = (P("seq", "tensor"), P("seq", "tensor"), P("seq", None), P("seq", None))
    out_specs = (P("seq", None), P("seq", None))
    return jax.shard_map(shards, mesh=mesh, in_specs=in_specs, out_specs=out_specs, check_vma=False)
```

profile of v0, /device:TPU:0, one launch (start us, length us, event | category | flops | bytes accessed | tf_op | source)
XLA Modules:
  0.0 555.9 jit_solution(9372963571637865610)
XLA Ops:
  7.2 4.0 copy.11
  11.7 4.1 collective-permute-done.2
  15.9 6.6 %maximum_select_fusion.2 = bf16[1024,2048]{0,1:T(8,128)(2,1)} fusion(bf16[512,2048]{0,1:T(8,128)(2,1)} %copy.11, bf16[512,2048]{0,1:T(8,128)(2,1)} %collective-permute-done.2, pred[]{:T(512)S(6)} %eq.15), kind=kLoop, calls=%fused_computation.66 | loop fusion | flops 18874368 | bytes 8388609 | tf_op jit(solution)/shard_map/jit(_where)/select_n | solution.py:67
  22.5 2.9 collective-permute-start.3
  25.7 3.9 copy.20
  43.0 96.5 %collective-permute-done.1 = bf16[1024,512]{0,1:T(8,128)(2,1)} collective-permute-done((bf16[1024,512]{0,1:T(8,128)(2,1)}, bf16[1024,512]{0,1:T(8,128)(2,1)}, u32[]{:S(2)}, u32[]{:S(2)}) %collective-permute-start.1) | collective-permute-done | bytes 1048608 | tf_op jit(solution)/shard_map/ppermute | solution.py:11
  139.5 3.7 fusion.47
  143.2 18.3 %collective-permute-done.5 = bf16[1024,512]{0,1:T(8,128)(2,1)} collective-permute-done((bf16[1024,512]{0,1:T(8,128)(2,1)}, bf16[1024,512]{0,1:T(8,128)(2,1)}, u32[]{:S(2)}, u32[]{:S(2)}) %collective-permute-start.5) | collective-permute-done | bytes 1048608 | tf_op jit(solution)/shard_map/ppermute | solution.py:11
  161.5 3.7 fusion.48
  165.1 4.9 maximum_select_fusion.4
  171.8 5.3 maximum_select_fusion.3
  177.1 5.0 maximum_select_fusion.5
  182.1 8.9 %fusion.44 = bf16[8,2048,256]{1,2,0:T(8,128)(2,1)} fusion(bf16[1024,8,256]{0,2,1:T(8,128)(2,1)S(1)} %maximum_select_fusion.3, bf16[1024,8,256]{0,2,1:T(8,128)(2,1)} %bitcast.19, pred[]{:T(512)S(6)} %eq.14), kind=kLoop, calls=%fused_computation.59 | loop fusion | flops 37748736 | bytes 16777216 | tf_op jit(solution)/shard_map/transpose | solution.py:32
  194.7 90.5 %while.24 = (s32[]{:T(128)}, f32[8,512,64]{1,2,0:T(8,128)}, f32[8,2048,64]{1,2,0:T(8,128)}, bf16[8,512,64]{1,2,0:T(8,128)(2,1)S(1)}, bf16[8,2048,64]{1,2,0:T(8,1...) while((s32[]{:T(128)}, f32[8,512,64]{1,2,0:T(8,128)}, ...), condition=%wide.region_5.6_spmd, body=%wide.region_0.5_spmd.sunk | while | flops 959444992 | bytes 34103380 | solution.py:39
  285.2 11.2 %fusion.45 = bf16[8,2048,256]{1,2,0:T(8,128)(2,1)} fusion(bf16[1024,8,256]{0,2,1:T(8,128)(2,1)} %maximum_select_fusion.5, bf16[1024,8,256]{0,2,1:T(8,128)(2,1)} %bitcast.33, pred[]{:T(512)S(6)} %eq.14), kind=kLoop, calls=%fused_computation.61 | loop fusion | flops 37748736 | bytes 16777216 | tf_op jit(solution)/shard_map/transpose | solution.py:32
  300.0 90.5 %while.25 = (s32[]{:T(128)}, f32[8,512,64]{1,2,0:T(8,128)}, f32[8,2048,64]{1,2,0:T(8,128)}, bf16[8,512,64]{1,2,0:T(8,128)(2,1)S(1)}, bf16[8,2048,64]{1,2,0:T(8,1...) while((s32[]{:T(128)}, f32[8,512,64]{1,2,0:T(8,128)}, ...), condition=%wide.region_11.12_spmd, body=%wide.region_6.11_spmd.sunk | while | flops 959444992 | bytes 34103380 | solution.py:39
  390.5 4.1 select_convert_fusion
  394.9 46.3 %collective-permute-done.8 = bf16[1024,1024]{0,1:T(8,128)(2,1)S(1)} collective-permute-done((bf16[1024,1024]{0,1:T(8,128)(2,1)S(1)}, bf16[1024,1024]{0,1:T(8,128)(2,1)S(1)}, u32[]{:S(2)}, u32[]{:S(2)}) %collective-permute-start.8) | collective-permute-done | bytes 2097184 | tf_op jit(solution)/shard_map/ppermute | solution.py:11
  441.2 4.2 convert_add_fusion
  449.0 2.9 fusion.49
  452.7 45.6 %all-gather.3.cloned.1.call-done = bf16[512,2048]{0,1:T(8,128)(2,1)} async-done(((bf16[512,512]{0,1:T(8,128)(2,1)}), bf16[512,2048]{0,1:T(8,128)(2,1)}) %all-gather.3.cloned.1.call-update) | async-done | bytes 2097168 | tf_op jit(solution)/shard_map/all_gather | solution.py:90
  498.3 3.9 copy.28
  502.2 42.9 %all-gather.5.cloned.1.call-done = bf16[512,2048]{0,1:T(8,128)(2,1)} async-done(((bf16[512,512]{0,1:T(8,128)(2,1)}), bf16[512,2048]{0,1:T(8,128)(2,1)}) %all-gather.5.cloned.1.call-update) | async-done | bytes 2097168 | tf_op jit(solution)/shard_map/all_gather | solution.py:91
  545.1 3.9 copy.29
  (135 shorter events, 208.6 us)
Async XLA Ops:
  7.2 18.2 %copy-start = (bf16[512,2048]{1,0:T(8,128)(2,1)S(1)}, bf16[512,2048]{1,0:T(8,128)(2,1)}, u32[]{:S(2)}) copy-start(bf16[512,2048]{1,0:T(8,128)(2,1)} %param.10) | copy-start | bytes 6291460
  7.2 491.1 %all-gather.3.cloned.1.call-start = ((), (), s32[]{:S(2)}) async-start(), calls=%async_computation | async-start | bytes 2621440 | tf_op jit(solution)/shard_map/all_gather | solution.py:90
  11.3 4.6 collective-permute-start.2
  22.5 159.6 %collective-permute-start.3 = (bf16[1024,2048]{0,1:T(8,128)(2,1)}, bf16[1024,2048]{0,1:T(8,128)(2,1)}, u32[]{:S(2)}, u32[]{:S(2)}) collective-permute-start(bf16[1024,2048]{0,1:T(8,128)(2,1)} %maximum_select_fusion.2), channel_id=1, source_target_pairs={{0,2},{1,3},{2,0},{3,1},{4,6},{5,7},{6,4},{7,5},{8,10},{9,11},{10,... | collective-permute-start | bytes 12582920 | tf_op jit(solution)/shard_map/ppermute | solution.py:11
  25.6 7.7 %collective-permute-start = (bf16[512,512]{0,1:T(8,128)(2,1)S(1)}, bf16[512,512]{0,1:T(8,128)(2,1)}, u32[]{:S(2)}, u32[]{:S(2)}) collective-permute-start(bf16[512,512]{0,1:T(8,128)(2,1)S(1)} %copy.38), channel_id=1, source_target_pairs={{0,1},{1,0},{2,3},{3,2},{4,5},{5,4},{6,7},{7,6},{8,9},{9,8},{10,11... | collective-permute-start | bytes 1572872 | tf_op jit(solution)/shard_map/ppermute | solution.py:11
  29.6 135.5 %collective-permute-start.6 = (bf16[512,2048]{0,1:T(8,128)(2,1)}, bf16[512,2048]{0,1:T(8,128)(2,1)S(1)}, u32[]{:S(2)}, u32[]{:S(2)}) collective-permute-start(bf16[512,2048]{0,1:T(8,128)(2,1)} %copy.20), channel_id=1, source_target_pairs={{0,1},{1,0},{2,3},{3,2},{4,5},{5,4},{6,7},{7,6},{8,9},{9,8},{10,11... | collective-permute-start | bytes 6291464 | tf_op jit(solution)/shard_map/ppermute | solution.py:11
  33.2 2.8 collective-permute-start.4
  35.9 103.6 %collective-permute-start.1 = (bf16[1024,512]{0,1:T(8,128)(2,1)}, bf16[1024,512]{0,1:T(8,128)(2,1)}, u32[]{:S(2)}, u32[]{:S(2)}) collective-permute-start(bf16[1024,512]{0,1:T(8,128)(2,1)} %maximum_select_fusion.8), channel_id=1, source_target_pairs={{0,2},{1,3},{2,0},{3,1},{4,6},{5,7},{6,4},{7,5},{8,10},{9,11},{10,... | collective-permute-start | bytes 3145736 | tf_op jit(solution)/shard_map/ppermute | solution.py:11
  36.0 0.8 copy-start.2
  38.1 123.4 %collective-permute-start.5 = (bf16[1024,512]{0,1:T(8,128)(2,1)}, bf16[1024,512]{0,1:T(8,128)(2,1)}, u32[]{:S(2)}, u32[]{:S(2)}) collective-permute-start(bf16[1024,512]{0,1:T(8,128)(2,1)} %maximum_select_fusion.10), channel_id=1, source_target_pairs={{0,2},{1,3},{2,0},{3,1},{4,6},{5,7},{6,4},{7,5},{8,10},{9,11},{10,... | collective-permute-start | bytes 3145736 | tf_op jit(solution)/shard_map/ppermute | solution.py:11
  170.1 115.1 %collective-permute-start.7 = (bf16[1024,2048]{0,1:T(8,128)(2,1)}, bf16[1024,2048]{0,1:T(8,128)(2,1)}, u32[]{:S(2)}, u32[]{:S(2)}) collective-permute-start(bf16[1024,2048]{0,1:T(8,128)(2,1)} %maximum_select_fusion.4), channel_id=1, source_target_pairs={{0,2},{1,3},{2,0},{3,1},{4,6},{5,7},{6,4},{7,5},{8,10},{9,11},{10,... | collective-permute-start | bytes 12582920 | tf_op jit(solution)/shard_map/ppermute | solution.py:11
  394.6 46.6 %collective-permute-start.8 = (bf16[1024,1024]{0,1:T(8,128)(2,1)S(1)}, bf16[1024,1024]{0,1:T(8,128)(2,1)S(1)}, u32[]{:S(2)}, u32[]{:S(2)}) collective-permute-start(bf16[1024,1024]{0,1:T(8,128)(2,1)S(1)} %select_convert_fusion), channel_id=1, source_target_pairs={{0,2},{1,3},{2,0},{3,1},{4,6},{5,7},{6,4},{7,5},{8,10},{9,11},{10,... | collective-permute-start | bytes 6291464 | tf_op jit(solution)/shard_map/ppermute | solution.py:11
  445.6 2.7 collective-permute-start.9
  451.9 93.2 %all-gather.5.cloned.1.call-start = ((), (), s32[]{:S(2)}) async-start(), calls=%async_computation.1 | async-start | bytes 2621440 | tf_op jit(solution)/shard_map/all_gather | solution.py:91
  452.7 96.4 %copy-start.1 = (bf16[512,2048]{1,0:T(8,128)(2,1)S(1)}, bf16[512,2048]{1,0:T(8,128)(2,1)}, u32[]{:S(2)}) copy-start(bf16[512,2048]{1,0:T(8,128)(2,1)} %param.10) | copy-start | bytes 6291460
Sparse Core Ops, SparseCore 0:
  452.0 46.2 all-gather.2
  500.5 44.6 all-gather.4
where the time goes:
time: 558 us; the launch traced here: 556 us
  waiting for transfers between devices  257 us (46%)
  other arithmetic  128 us (23%)
  matrix products  121 us (22%)
  local copies, waits for them, and re-layouts  27.2 us (5%)
  between operations  14.2 us (3%)
  starting transfers between devices  8.22 us (1%)
    ppermute x10, waiting for transfers between devices, from_partner(): lax.ppermute(array, axis, [(i, i ^ 1 << distance) for i in range(lax.axis...  168 us
    all_gather x1, waiting for transfers between devices, shards(): lax.all_gather(head_q, 'tensor', axis=1, tiled=True)  45.6 us
    all_gather x1, waiting for transfers between devices, shards(): lax.all_gather(head_v, 'tensor', axis=1, tiled=True)  42.9 us
    dot_general x16, matrix products, head_terms(): query_grad = jnp.dot(coef, stud_key, preferred_element_type=jnp.float32)  37.8 us
    dot_general x16, matrix products, head_terms(): jnp.dot(teach_query, teach_key.T, preferred_element_type=jnp.float32)  34.1 us
    convert_element_type x16, other arithmetic, head_terms(): (256.0 * stud_dim ** (-0.5) * (stud_prob - teach_prob)).astype(jnp.bfloat16)  31.4 us
    select_n x8, other arithmetic, shards(): jnp.where(upper_half, jnp.concatenate([theirs, mine], 0), jnp.concatenate...  28.7 us
    reduce_sum x16, other arithmetic, head_terms(): stud_prob = jax.nn.softmax(stud_scores, axis=-1)  28.5 us
  transfers between devices with their start and end apart: 12, of which 7 were waited for; matrix products, arithmetic and copies ran while one was open for 26% of the time, Pallas kernels for 0%

commit v1 on v0

--- a/solution.py
+++ b/solution.py
@@ -1,3 +1,4 @@
+import functools
 import jax
 import jax.numpy as jnp
 from jax import lax
@@ -5,6 +6,34 @@
 
 HEADS = 32
 SEQS = 2
+
+
+def leaf_draft(body, comm_axis):
+    arrivals = []
+    plain, last, piece_now = (lax.psum(1, comm_axis), lax.axis_index(comm_axis), body.shape[1])
+    for idx in range(plain):
+        arrivals.append((idx, (idx + 1) % plain))
+    slots = []
+    for idx in range(plain):
+        slots.append((idx, (idx - 1) % plain))
+    oldest = jnp.zeros((*body.shape[:1], plain * piece_now, *body.shape[2:]), body.dtype)
+    oldest = lax.dynamic_update_slice_in_dim(oldest, body, last * piece_now, axis=1)
+    t_next = local_next = body
+    out_arr = plain // 2
+    for ix in range(1, out_arr + 1):
+        t_next = lax.ppermute(t_next, comm_axis, arrivals)
+        oldest = lax.dynamic_update_slice_in_dim(
+            oldest, t_next, (last - ix) % plain * piece_now, axis=1
+        )
+        if ix < plain - out_arr:
+            local_next = lax.ppermute(local_next, comm_axis, slots)
+            oldest = lax.dynamic_update_slice_in_dim(
+                oldest, local_next, (last + ix) % plain * piece_now, axis=1
+            )
+    return oldest
+
+
+slots_tell = functools.partial(leaf_draft, comm_axis="tensor")
 
 
 def from_partner(array, axis, distance):
@@ -86,10 +115,7 @@
         )
     head_q = (q_query + returned[:, :own_width]).astype(jnp.bfloat16)
     head_v = (v_query + returned[:, own_width:]).astype(jnp.bfloat16)
-    full_q, full_v = (
-        lax.all_gather(head_q, "tensor", axis=1, tiled=True),
-        lax.all_gather(head_v, "tensor", axis=1, tiled=True),
-    )
+    full_q, full_v = (lax.all_gather(head_q, "tensor", axis=1, tiled=True), slots_tell(head_v))
     return (full_q, full_v)
 
 

time: 558 us -> 537 us (0.962)
  waiting for transfers between devices: 257 us -> 216 us
  starting transfers between devices: 8.22 us -> 23.2 us
    all_gather x1 -> x0, waiting for transfers between devices: 42.9 us -> none  [shards(): lax.all_gather(head_v, 'tensor', axis=1, tiled=True)]
    ppermute x0 -> x3, waiting for transfers between devices: none -> 42.8 us  [the longest x2 23.2 us: leaf_draft(): t_next = lax.ppermute(t_next, comm_axis, arrivals)]
    all_gather x1, waiting for transfers between devices: 45.6 us -> 5.57 us  [shards(): lax.all_gather(head_q, 'tensor', axis=1, tiled=True)]
    ppermute x0 -> x3, starting transfers between devices: none -> 15 us  [the longest x2 12.7 us: leaf_draft(): t_next = lax.ppermute(t_next, comm_axis, arrivals)]
    unnamed x12 -> x11, local copies, waits for them, and re-layouts: 18.1 us -> 14.1 us
  transfers between devices with their start and end apart: 12 -> 14, of which waited for: 7 -> 9; matrix products, arithmetic and copies ran while one was open for 26% -> 28% of each run, Pallas kernels for 0% -> 0%
where the time goes in v1:
time: 537 us; the launch traced here: 535 us
  waiting for transfers between devices  216 us (40%)
  other arithmetic  128 us (24%)
  matrix products  121 us (23%)
  local copies, waits for them, and re-layouts  32.3 us (6%)
  starting transfers between devices  23.2 us (4%)
  between operations  14.2 us (3%)
    ppermute x10, waiting for transfers between devices, from_partner(): lax.ppermute(array, axis, [(i, i ^ 1 << distance) for i in range(lax.axis...  168 us
    dot_general x16, matrix products, head_terms(): query_grad = jnp.dot(coef, stud_key, preferred_element_type=jnp.float32)  37.8 us
    dot_general x16, matrix products, head_terms(): jnp.dot(teach_query, teach_key.T, preferred_element_type=jnp.float32)  34.1 us
    convert_element_type x16, other arithmetic, head_terms(): (256.0 * stud_dim ** (-0.5) * (stud_prob - teach_prob)).astype(jnp.bfloat16)  31.4 us
    select_n x8, other arithmetic, shards(): jnp.where(upper_half, jnp.concatenate([theirs, mine], 0), jnp.concatenate...  28.7 us
    reduce_sum x16, other arithmetic, head_terms(): stud_prob = jax.nn.softmax(stud_scores, axis=-1)  28.5 us
    dot_general x16, matrix products, head_terms(): jnp.dot(stud_query, stud_key.T, preferred_element_type=jnp.float32)  28.2 us
    ppermute x2, waiting for transfers between devices, leaf_draft(): t_next = lax.ppermute(t_next, comm_axis, arrivals)  23.2 us
  transfers between devices with their start and end apart: 14, of which 9 were waited for; matrix products, arithmetic and copies ran while one was open for 28% of the time, Pallas kernels for 0%

profile of v1, /device:TPU:0, one launch (start us, length us, event | category | flops | bytes accessed | tf_op | source)
XLA Modules:
  0.0 535.1 jit_solution(8413722543100575426)
XLA Ops:
  7.2 4.0 copy.11
  11.7 4.1 collective-permute-done.2
  15.9 6.6 %maximum_select_fusion.2 = bf16[1024,2048]{0,1:T(8,128)(2,1)} fusion(bf16[512,2048]{0,1:T(8,128)(2,1)} %copy.11, bf16[512,2048]{0,1:T(8,128)(2,1)} %collective-permute-done.2, pred[]{:T(512)S(6)} %eq.18), kind=kLoop, calls=%fused_computation.66 | loop fusion | flops 18874368 | bytes 8388609 | tf_op jit(solution)/shard_map/jit(_where)/select_n | solution.py:96
  25.7 3.9 copy.20
  43.0 96.5 %collective-permute-done.1 = bf16[1024,512]{0,1:T(8,128)(2,1)} collective-permute-done((bf16[1024,512]{0,1:T(8,128)(2,1)}, bf16[1024,512]{0,1:T(8,128)(2,1)}, u32[]{:S(2)}, u32[]{:S(2)}) %collective-permute-start.1) | collective-permute-done | bytes 1048608 | tf_op jit(solution)/shard_map/ppermute | solution.py:40
  139.5 3.7 fusion.47
  143.2 18.3 %collective-permute-done.5 = bf16[1024,512]{0,1:T(8,128)(2,1)} collective-permute-done((bf16[1024,512]{0,1:T(8,128)(2,1)}, bf16[1024,512]{0,1:T(8,128)(2,1)}, u32[]{:S(2)}, u32[]{:S(2)}) %collective-permute-start.5) | collective-permute-done | bytes 1048608 | tf_op jit(solution)/shard_map/ppermute | solution.py:40
  161.5 3.7 fusion.48
  165.1 4.9 maximum_select_fusion.4
  171.8 5.3 maximum_select_fusion.3
  177.1 5.0 maximum_select_fusion.5
  182.1 8.9 %fusion.44 = bf16[8,2048,256]{1,2,0:T(8,128)(2,1)} fusion(bf16[1024,8,256]{0,2,1:T(8,128)(2,1)S(1)} %maximum_select_fusion.3, bf16[1024,8,256]{0,2,1:T(8,128)(2,1)} %bitcast.19, pred[]{:T(512)S(6)} %eq.17), kind=kLoop, calls=%fused_computation.59 | loop fusion | flops 37748736 | bytes 16777216 | tf_op jit(solution)/shard_map/transpose | solution.py:61
  194.7 90.5 %while.24 = (s32[]{:T(128)}, f32[8,512,64]{1,2,0:T(8,128)}, f32[8,2048,64]{1,2,0:T(8,128)}, bf16[8,512,64]{1,2,0:T(8,128)(2,1)S(1)}, bf16[8,2048,64]{1,2,0:T(8,1...) while((s32[]{:T(128)}, f32[8,512,64]{1,2,0:T(8,128)}, ...), condition=%wide.region_5.6_spmd, body=%wide.region_0.5_spmd.sunk | while | flops 959444992 | bytes 34103380 | solution.py:68
  285.2 11.2 %fusion.45 = bf16[8,2048,256]{1,2,0:T(8,128)(2,1)} fusion(bf16[1024,8,256]{0,2,1:T(8,128)(2,1)} %maximum_select_fusion.5, bf16[1024,8,256]{0,2,1:T(8,128)(2,1)} %bitcast.33, pred[]{:T(512)S(6)} %eq.17), kind=kLoop, calls=%fused_computation.61 | loop fusion | flops 37748736 | bytes 16777216 | tf_op jit(solution)/shard_map/transpose | solution.py:61
  300.0 90.5 %while.25 = (s32[]{:T(128)}, f32[8,512,64]{1,2,0:T(8,128)}, f32[8,2048,64]{1,2,0:T(8,128)}, bf16[8,512,64]{1,2,0:T(8,128)(2,1)S(1)}, bf16[8,2048,64]{1,2,0:T(8,1...) while((s32[]{:T(128)}, f32[8,512,64]{1,2,0:T(8,128)}, ...), condition=%wide.region_11.12_spmd, body=%wide.region_6.11_spmd.sunk | while | flops 959444992 | bytes 34103380 | solution.py:68
  390.5 4.1 select_convert_fusion
  394.9 46.3 %collective-permute-done.8 = bf16[1024,1024]{0,1:T(8,128)(2,1)S(1)} collective-permute-done((bf16[1024,1024]{0,1:T(8,128)(2,1)S(1)}, bf16[1024,1024]{0,1:T(8,128)(2,1)S(1)}, u32[]{:S(2)}, u32[]{:S(2)}) %collective-permute-start.8) | collective-permute-done | bytes 2097184 | tf_op jit(solution)/shard_map/ppermute | solution.py:40
  441.2 4.5 convert_add_fusion
  455.8 16.7 %collective-permute-done.10 = bf16[512,512]{0,1:T(8,128)(2,1)} collective-permute-done((bf16[512,512]{0,1:T(8,128)(2,1)S(1)}, bf16[512,512]{0,1:T(8,128)(2,1)}, u32[]{:S(2)}, u32[]{:S(2)}) %collective-permute-start.10) | collective-permute-done | bytes 524320 | tf_op jit(solution)/shard_map/ppermute | solution.py:24
  472.5 11.1 %collective-permute-start.12 = (bf16[512,512]{0,1:T(8,128)(2,1)}, bf16[512,512]{0,1:T(8,128)(2,1)}, u32[]{:S(2)}, u32[]{:S(2)}) collective-permute-start(bf16[512,512]{0,1:T(8,128)(2,1)} %collective-permute-done.10), channel_id=1, source_target_pairs={{0,8},{8,16},{16,24},{24,0},{1,9},{9,17},{17,25},{25,1},{2,10},{10... | collective-permute-start | bytes 1572872 | tf_op jit(solution)/shard_map/ppermute | solution.py:24
  487.5 19.6 %collective-permute-done.11 = bf16[512,512]{0,1:T(8,128)(2,1)} collective-permute-done((bf16[512,512]{0,1:T(8,128)(2,1)S(1)}, bf16[512,512]{0,1:T(8,128)(2,1)}, u32[]{:S(2)}, u32[]{:S(2)}) %collective-permute-start.11) | collective-permute-done | bytes 524320 | tf_op jit(solution)/shard_map/ppermute | solution.py:29
  510.2 6.5 %collective-permute-done.12 = bf16[512,512]{0,1:T(8,128)(2,1)} collective-permute-done((bf16[512,512]{0,1:T(8,128)(2,1)}, bf16[512,512]{0,1:T(8,128)(2,1)}, u32[]{:S(2)}, u32[]{:S(2)}) %collective-permute-start.12) | collective-permute-done | bytes 524320 | tf_op jit(solution)/shard_map/ppermute | solution.py:24
  518.8 5.6 %all-gather.2.cloned.1.call-done = bf16[512,2048]{0,1:T(8,128)(2,1)} async-done(((bf16[512,512]{0,1:T(8,128)(2,1)}), bf16[512,2048]{0,1:T(8,128)(2,1)}) %all-gather.2.cloned.1.call-update) | async-done | bytes 2097168 | tf_op jit(solution)/shard_map/all_gather | solution.py:118
  524.4 3.9 copy.32
  (146 shorter events, 226.3 us)
Async XLA Ops:
  7.2 18.2 %copy-start = (bf16[512,2048]{1,0:T(8,128)(2,1)S(1)}, bf16[512,2048]{1,0:T(8,128)(2,1)}, u32[]{:S(2)}) copy-start(bf16[512,2048]{1,0:T(8,128)(2,1)} %param.10) | copy-start | bytes 6291460
  7.2 517.2 %all-gather.2.cloned.1.call-start = ((), (), s32[]{:S(2)}) async-start(), calls=%async_computation | async-start | bytes 2621440 | tf_op jit(solution)/shard_map/all_gather | solution.py:118
  11.3 4.6 collective-permute-start.2
  22.5 159.6 %collective-permute-start.3 = (bf16[1024,2048]{0,1:T(8,128)(2,1)}, bf16[1024,2048]{0,1:T(8,128)(2,1)}, u32[]{:S(2)}, u32[]{:S(2)}) collective-permute-start(bf16[1024,2048]{0,1:T(8,128)(2,1)} %maximum_select_fusion.2), channel_id=1, source_target_pairs={{0,2},{1,3},{2,0},{3,1},{4,6},{5,7},{6,4},{7,5},{8,10},{9,11},{10,... | collective-permute-start | bytes 12582920 | tf_op jit(solution)/shard_map/ppermute | solution.py:40
  25.6 7.7 %collective-permute-start = (bf16[512,512]{0,1:T(8,128)(2,1)S(1)}, bf16[512,512]{0,1:T(8,128)(2,1)}, u32[]{:S(2)}, u32[]{:S(2)}) collective-permute-start(bf16[512,512]{0,1:T(8,128)(2,1)S(1)} %copy.41), channel_id=1, source_target_pairs={{0,1},{1,0},{2,3},{3,2},{4,5},{5,4},{6,7},{7,6},{8,9},{9,8},{10,11... | collective-permute-start | bytes 1572872 | tf_op jit(solution)/shard_map/ppermute | solution.py:40
  29.6 135.5 %collective-permute-start.6 = (bf16[512,2048]{0,1:T(8,128)(2,1)}, bf16[512,2048]{0,1:T(8,128)(2,1)S(1)}, u32[]{:S(2)}, u32[]{:S(2)}) collective-permute-start(bf16[512,2048]{0,1:T(8,128)(2,1)} %copy.20), channel_id=1, source_target_pairs={{0,1},{1,0},{2,3},{3,2},{4,5},{5,4},{6,7},{7,6},{8,9},{9,8},{10,11... | collective-permute-start | bytes 6291464 | tf_op jit(solution)/shard_map/ppermute | solution.py:40
  33.2 2.8 collective-permute-start.4
  35.9 103.6 %collective-permute-start.1 = (bf16[1024,512]{0,1:T(8,128)(2,1)}, bf16[1024,512]{0,1:T(8,128)(2,1)}, u32[]{:S(2)}, u32[]{:S(2)}) collective-permute-start(bf16[1024,512]{0,1:T(8,128)(2,1)} %maximum_select_fusion.8), channel_id=1, source_target_pairs={{0,2},{1,3},{2,0},{3,1},{4,6},{5,7},{6,4},{7,5},{8,10},{9,11},{10,... | collective-permute-start | bytes 3145736 | tf_op jit(solution)/shard_map/ppermute | solution.py:40
  36.0 0.8 copy-start.2
  38.1 123.4 %collective-permute-start.5 = (bf16[1024,512]{0,1:T(8,128)(2,1)}, bf16[1024,512]{0,1:T(8,128)(2,1)}, u32[]{:S(2)}, u32[]{:S(2)}) collective-permute-start(bf16[1024,512]{0,1:T(8,128)(2,1)} %maximum_select_fusion.10), channel_id=1, source_target_pairs={{0,2},{1,3},{2,0},{3,1},{4,6},{5,7},{6,4},{7,5},{8,10},{9,11},{10,... | collective-permute-start | bytes 3145736 | tf_op jit(solution)/shard_map/ppermute | solution.py:40
  170.1 115.1 %collective-permute-start.7 = (bf16[1024,2048]{0,1:T(8,128)(2,1)}, bf16[1024,2048]{0,1:T(8,128)(2,1)}, u32[]{:S(2)}, u32[]{:S(2)}) collective-permute-start(bf16[1024,2048]{0,1:T(8,128)(2,1)} %maximum_select_fusion.4), channel_id=1, source_target_pairs={{0,2},{1,3},{2,0},{3,1},{4,6},{5,7},{6,4},{7,5},{8,10},{9,11},{10,... | collective-permute-start | bytes 12582920 | tf_op jit(solution)/shard_map/ppermute | solution.py:40
  394.6 46.6 %collective-permute-start.8 = (bf16[1024,1024]{0,1:T(8,128)(2,1)S(1)}, bf16[1024,1024]{0,1:T(8,128)(2,1)S(1)}, u32[]{:S(2)}, u32[]{:S(2)}) collective-permute-start(bf16[1024,1024]{0,1:T(8,128)(2,1)S(1)} %select_convert_fusion), channel_id=1, source_target_pairs={{0,2},{1,3},{2,0},{3,1},{4,6},{5,7},{6,4},{7,5},{8,10},{9,11},{10,... | collective-permute-start | bytes 6291464 | tf_op jit(solution)/shard_map/ppermute | solution.py:40
  445.9 2.7 collective-permute-start.9
  452.0 20.6 %collective-permute-start.10 = (bf16[512,512]{0,1:T(8,128)(2,1)S(1)}, bf16[512,512]{0,1:T(8,128)(2,1)}, u32[]{:S(2)}, u32[]{:S(2)}) collective-permute-start(bf16[512,512]{0,1:T(8,128)(2,1)S(1)} %get-tuple-element.138), channel_id=1, source_target_pairs={{0,8},{8,16},{16,24},{24,0},{1,9},{9,17},{17,25},{25,1},{2,10},{10... | collective-permute-start | bytes 1572872 | tf_op jit(solution)/shard_map/ppermute | solution.py:24
  453.6 53.6 %collective-permute-start.11 = (bf16[512,512]{0,1:T(8,128)(2,1)S(1)}, bf16[512,512]{0,1:T(8,128)(2,1)}, u32[]{:S(2)}, u32[]{:S(2)}) collective-permute-start(bf16[512,512]{0,1:T(8,128)(2,1)S(1)} %get-tuple-element.138), channel_id=1, source_target_pairs={{0,24},{8,0},{16,8},{24,16},{1,25},{9,1},{17,9},{25,17},{2,26},{10... | collective-permute-start | bytes 1572872 | tf_op jit(solution)/shard_map/ppermute | solution.py:29
  472.5 44.2 %collective-permute-start.12 = (bf16[512,512]{0,1:T(8,128)(2,1)}, bf16[512,512]{0,1:T(8,128)(2,1)}, u32[]{:S(2)}, u32[]{:S(2)}) collective-permute-start(bf16[512,512]{0,1:T(8,128)(2,1)} %collective-permute-done.10), channel_id=1, source_target_pairs={{0,8},{8,16},{16,24},{24,0},{1,9},{9,17},{17,25},{25,1},{2,10},{10... | collective-permute-start | bytes 1572872 | tf_op jit(solution)/shard_map/ppermute | solution.py:24
  507.1 21.2 %copy-start.1 = (bf16[512,2048]{1,0:T(8,128)(2,1)S(1)}, bf16[512,2048]{1,0:T(8,128)(2,1)}, u32[]{:S(2)}) copy-start(bf16[512,2048]{1,0:T(8,128)(2,1)} %param.10) | copy-start | bytes 6291460
Sparse Core Ops, SparseCore 0:
  452.1 72.2 all-gather.1
